TPU v7x, 256 devices: a whole 4x4x8 slice. The times are simulated.
256 devices in a mesh: pb: 16 (over x_lo, z), ka: 16 (over x_hi, y, core).
Axes of the slice: x: 4 (x_hi: 2, x_lo: 2; x = x_hi * 2 + x_lo), y: 4, z: 8, core: 2. Of those that a mesh axis runs over, the one named last changes fastest.
Arguments:
- query_saved: bfloat16 [8192, 1024], P(('pb', 'ka')), may hold values from -6 to 6
- key_saved: bfloat16 [16384, 1024], P(('ka', 'pb')), may hold values from -6 to 6
- value_saved: bfloat16 [16384, 1024], P(('ka', 'pb')), may hold values from -6 to 6
- out_grad: bfloat16 [8192, 1024], P(('pb', 'ka')), may hold values from -768 to 768
- log_norm: bfloat16 [16, 8192], P(None, ('pb', 'ka')), as said below
- row_delta: bfloat16 [16, 8192], P(None, ('pb', 'ka')), may hold values from -1536 to 1536
- weight_query: bfloat16 [1024, 1024], replicated, may hold values from -0.1875 to 0.1875
- weight_key: bfloat16 [1024, 1024], replicated, may hold values from -0.1875 to 0.1875
- weight_value: bfloat16 [1024, 1024], replicated, may hold values from -0.1875 to 0.1875
Outputs:
- dx_query: bfloat16 [8192, 1024], P(('pb', 'ka'))
- dx_keyvalue: bfloat16 [16384, 1024], P(('ka', 'pb'))
Inputs may be any that keep to these rules, and one draw needn't show every extreme that they name: `log_norm`: each entry lies within 2 of 0.5 plus the natural logarithm of 16384.
All inputs are finite; a program needn't handle non-finite values.
Results may differ from a plain program's by a relative error of at most 0.008.
Values may be sent and summed in bfloat16 or wider, within the bound.
A program may use at most 128 MiB of HBM per device.

v0:
```python
import jax
import jax.numpy as jnp
from jax import lax
from jax.sharding import PartitionSpec as P

HEAD_DIM = 64


def turned_gather(arrays, axis, dims):
    turned = [jnp.moveaxis(a, dim, 0) for a, dim in zip(arrays, dims)]
    both = jnp.concatenate([t.reshape(len(t), -1) for t in turned], axis=1)
    whole, at, outs = (lax.all_gather(both, axis, axis=0, tiled=True), 0, [])
    for t, dim in zip(turned, dims):
        share = whole[:, at : at + t[0].size].reshape(-1, *t.shape[1:])
        outs.append(jnp.moveaxis(share, 0, dim))
        at += t[0].size
    return tuple(outs)


def in_one_piece(arrays, axis, dim, along):
    both = jnp.concatenate(arrays, axis=along)
    whole, at, outs = (lax.all_gather(both, axis, axis=dim, tiled=True), 0, [])
    for a in arrays:
        outs.append(lax.slice_in_dim(whole, at, at + a.shape[along], axis=along))
        at += a.shape[along]
    return tuple(outs)


def cut_along(array, dim, size):
    before, after = (array.shape[:dim], array.shape[dim + 1 :])
    return jnp.moveaxis(array.reshape(*before, size, -1, *after), dim, 0)


def summed_on_arrival(array, axis, dim):
    pieces = cut_along(array, dim, lax.axis_size(axis))
    arrived = lax.all_to_all(pieces, axis, split_axis=0, concat_axis=0, tiled=True)
    return arrived.sum(axis=0)


def project(grads, weights):
    contract = (((1,), (1,)), ((), ()))
    upper = grads.astype(jnp.bfloat16)
    lower = (grads - upper.astype(jnp.float32)).astype(jnp.bfloat16)
    first = lax.dot_general(upper, weights, contract, preferred_element_type=jnp.float32)
    return first + lax.dot_general(lower, weights, contract, preferred_element_type=jnp.float32)


def local(
    query_saved,
    key_saved,
    value_saved,
    out_grad,
    log_norm,
    row_delta,
    weight_query,
    weight_key,
    weight_value,
):
    query_block, grad_out_block, norm_block, delta_block = turned_gather(
        (query_saved, out_grad, log_norm, row_delta), "ka", (0, 0, 1, 1)
    )
    key_block, value_block = in_one_piece((key_saved, value_saved), "pb", 0, 1)
    query_rows = query_block.shape[0]
    key_rows = key_block.shape[0]
    model_width = query_block.shape[1]
    pair_width = 2 * HEAD_DIM
    pair_count = model_width // pair_width
    score_scale = 1.0 / HEAD_DIM**0.5

    def columns(source, row_count, column):
        return lax.dynamic_slice_in_dim(source, column, pair_width, 1).reshape(
            row_count, 2, HEAD_DIM
        )

    def head_pair(pair_index, totals):
        grad_query, grad_key, grad_value = totals
        column = pair_index * pair_width
        queries = columns(query_block, query_rows, column)
        grads_out = columns(grad_out_block, query_rows, column)
        keys_pair = columns(key_block, key_rows, column)
        values_pair = columns(value_block, key_rows, column)
        norm_pair = lax.dynamic_slice_in_dim(norm_block, pair_index * 2, 2, 0).astype(jnp.float32)
        delta_pair = lax.dynamic_slice_in_dim(delta_block, pair_index * 2, 2, 0).astype(jnp.float32)
        scores = (
            jnp.einsum("qhd,khd->hqk", queries, keys_pair, preferred_element_type=jnp.float32)
            * score_scale
        )
        probs = jnp.exp(scores - norm_pair[:, :, None])
        probs_b = probs.astype(jnp.bfloat16)
        grad_probs = jnp.einsum(
            "qhd,khd->hqk", grads_out, values_pair, preferred_element_type=jnp.float32
        )
        grad_scores = probs * (grad_probs - delta_pair[:, :, None])
        grad_scores_b = grad_scores.astype(jnp.bfloat16)
        value_part = jnp.einsum(
            "hqk,qhd->khd", probs_b, grads_out, preferred_element_type=jnp.float32
        )
        key_part = (
            jnp.einsum("hqk,qhd->khd", grad_scores_b, queries, preferred_element_type=jnp.float32)
            * score_scale
        )
        query_part = (
            jnp.einsum("hqk,khd->qhd", grad_scores_b, keys_pair, preferred_element_type=jnp.float32)
            * score_scale
        )
        grad_query = lax.dynamic_update_slice_in_dim(
            grad_query, query_part.reshape(query_rows, pair_width), column, 1
        )
        grad_key = lax.dynamic_update_slice_in_dim(
            grad_key, key_part.reshape(key_rows, pair_width), column, 1
        )
        grad_value = lax.dynamic_update_slice_in_dim(
            grad_value, value_part.reshape(key_rows, pair_width), column, 1
        )
        return (grad_query, grad_key, grad_value)

    start_totals = (
        jnp.zeros((query_rows, model_width), jnp.float32),
        jnp.zeros((key_rows, model_width), jnp.float32),
        jnp.zeros((key_rows, model_width), jnp.float32),
    )
    grad_query, grad_key, grad_value = lax.fori_loop(0, pair_count, head_pair, start_totals)
    query_owned = summed_on_arrival(grad_query, "ka", 0)
    dx_query = project(query_owned, weight_query).astype(jnp.bfloat16)
    combined = lax.psum_scatter(
        project(grad_key, weight_key) + project(grad_value, weight_value),
        "pb",
        scatter_dimension=0,
        tiled=True,
    )
    return (dx_query, combined.astype(jnp.bfloat16))


def solution(mesh):
    in_specs = (
        P(("pb", "ka"), None),
        P(("ka", "pb"), None),
        P(("ka", "pb"), None),
        P(("pb", "ka"), None),
        P(None, ("pb", "ka")),
        P(None, ("pb", "ka")),
        P(),
        P(),
        P(),
    )
    out_specs = (P(("pb", "ka"), None), P(("ka", "pb"), None))
    return jax.shard_map(local, mesh=mesh, in_specs=in_specs, out_specs=out_specs, check_vma=False)
```

profile of v0, /device:TPU:1, one launch (start us, length us, event | category | flops | bytes accessed | tf_op | source)
XLA Modules:
  0.0 404.5 jit_solution(9012038801444928533)
XLA Ops:
  12.4 55.4 %all-gather.5.cloned.1.call-done = bf16[512,2080]{1,0:T(8,128)(2,1)} async-done(((bf16[32,2080]{1,0:T(8,128)(2,1)}), bf16[512,2080]{1,0:T(8,128)(2,1)}) %all-gather.5.cloned.1.call-update) | async-done | bytes 2129936 | tf_op jit(solution)/shard_map/all_gather | solution.py:12
  69.0 3.1 fusion.20
  72.1 62.5 %all-gather.3.cloned.1.call-done = bf16[1024,2048]{1,0:T(8,128)(2,1)} async-done(((bf16[64,2048]{1,0:T(8,128)(2,1)}), bf16[1024,2048]{1,0:T(8,128)(2,1)}) %all-gather.3.cloned.1.call-update) | async-done | bytes 4194320 | tf_op jit(solution)/shard_map/all_gather | solution.py:22
  134.6 4.6 %fusion.19 = (bf16[1024,1024]{1,0:T(8,128)(2,1)}, bf16[1024,1024]{1,0:T(8,128)(2,1)}) fusion(bf16[1024,2048]{1,0:T(8,128)(2,1)} %all-gather.3.cloned.1.call-done), kind=kLoop, calls=%fused_computation.39 | loop fusion | bytes 8388608 | tf_op jit(solution)/shard_map/slice | solution.py:24
  145.7 145.1 %while.17 = (s32[]{:T(128)}, f32[512,1024]{1,0:T(8,128)}, f32[1024,1024]{0,1:T(8,128)}, f32[1024,1024]{0,1:T(8,128)}, bf16[1024,1024]{1,0:T(8,128)(2,1)}, /*inde...) while((s32[]{:T(128)}, f32[512,1024]{1,0:T(8,128)}, ...), condition=%wide.region_1.0_spmd, body=%wide.region_0.0_spmd.sunk | while | flops 679675904 | bytes 44589392 | solution.py:122
  147.9 2.7 fusion.61
  152.8 3.4 multiply_convert_fusion.2
  159.2 3.1 fusion.64
  166.0 2.7 fusion.61
  171.0 3.4 multiply_convert_fusion.2
  177.3 3.1 fusion.64
  184.2 2.7 fusion.61
  189.1 3.4 multiply_convert_fusion.2
  195.4 3.1 fusion.64
  202.3 2.7 fusion.61
  207.2 3.4 multiply_convert_fusion.2
  213.6 3.1 fusion.64
  220.4 2.7 fusion.61
  225.3 3.4 multiply_convert_fusion.2
  231.7 3.1 fusion.64
  243.5 3.4 multiply_convert_fusion.2
  249.8 3.1 fusion.64
  256.6 2.7 fusion.61
  261.6 3.4 multiply_convert_fusion.2
  267.9 3.1 fusion.64
  274.8 2.7 fusion.61
  279.7 3.4 multiply_convert_fusion.2
  286.1 3.1 fusion.64
  290.8 4.7 %fusion.14 = f32[1024,1024]{1,0:T(8,128)S(1)} fusion(bf16[1024,1024]{1,0:T(8,128)(2,1)S(1)} %copy-done, f32[1024,1024]{0,1:T(8,128)} %get-tuple-element.174), kind=kOutput, calls=%fused_computation.30 | convolution fusion | flops 2148532224 | bytes 10485760 | tf_op jit(solution)/shard_map/dot_general | solution.py:44
  300.8 4.4 %add_add_fusion = f32[1024,1024]{1,0:T(8,128)} fusion(f32[1024,1024]{1,0:T(8,128)S(1)} %fusion.9, f32[1024,1024]{1,0:T(8,128)S(1)} %fusion.14, f32[1024,1024]{1,0:T(8,128)S(1)} %fusion.8, bf16[1024,1024]{1,0:T(8,128)(2,1)S(1)} %copy-done.5, f32[1024,1024]{0,1:T(8,128)S(1)} %copy-done.3), kind=kOutput, calls=%fused_computation.20 | convolution fusion | flops 2151677952 | bytes 23068672 | tf_op jit(solution)/shard_map/dot_general | solution.py:44
  305.2 84.1 %all_to_all.5 = f32[16,32,1024]{2,1,0:T(8,128)} all-to-all(f32[16,32,1024]{2,1,0:T(8,128)} %bitcast.77), channel_id=1, replica_groups=mesh['pb'=16,'ka'=16] {'ka'}, dimensions={0} | all-to-all | bytes 4194304 | tf_op jit(solution)/shard_map/all_to_all | solution.py:36
  393.4 3.0 fusion.10
  (183 shorter events, 97.5 us)
Async XLA Ops:
  7.2 283.6 %copy-start = (bf16[1024,1024]{1,0:T(8,128)(2,1)S(1)}, bf16[1024,1024]{1,0:T(8,128)(2,1)}, u32[]{:S(2)}) copy-start(bf16[1024,1024]{1,0:T(8,128)(2,1)} %param.18) | copy-start | bytes 6291460
  7.2 60.6 %all-gather.5.cloned.1.call-start = ((), (), s32[]{:S(2)}) async-start(), calls=%async_computation.3 | async-start | bytes 2367488 | tf_op jit(solution)/shard_map/all_gather | solution.py:12
  10.5 124.0 %all-gather.3.cloned.1.call-start = ((), (), s32[]{:S(2)}) async-start(), calls=%async_computation.2 | async-start | bytes 4456448 | tf_op jit(solution)/shard_map/all_gather | solution.py:22
  12.3 384.0 %reduce-scatter.2.cloned.1.call-start = ((), (), s32[]{:S(2)}) async-start(), calls=%async_computation.4 | async-start | bytes 4456448 | tf_op jit(solution)/shard_map/reduce_scatter | solution.py:125
  156.2 1.3 copy-start.1
  158.4 3.9 copy-start.2
  174.3 1.3 copy-start.1
  176.5 3.9 copy-start.2
  192.4 1.3 copy-start.1
  194.7 3.8 copy-start.2
  210.6 1.3 copy-start.1
  212.8 3.9 copy-start.2
  228.7 1.3 copy-start.1
  230.9 3.8 copy-start.2
  246.8 1.3 copy-start.1
  249.0 3.8 copy-start.2
  264.9 1.3 copy-start.1
  267.2 3.9 copy-start.2
  283.1 1.3 copy-start.1
  285.3 3.9 copy-start.2
  290.8 4.7 %copy-start.4 = (f32[1024,1024]{0,1:T(8,128)S(1)}, f32[1024,1024]{0,1:T(8,128)}, u32[]{:S(2)}) copy-start(f32[1024,1024]{0,1:T(8,128)} %get-tuple-element.174) | copy-start | bytes 12582916
  295.5 2.4 copy-start.3
  295.5 2.9 copy-start.5
Sparse Core Ops, SparseCore 0:
  10.8 56.9 all-gather.4
  69.6 64.9 all-gather.2
  305.3 78.8 reduce-scatter.1
where the time goes:
time: 406 us; the launch traced here: 405 us
  waiting for transfers between devices  118 us (29%)
  matrix products  102 us (25%)
  blocking collectives  84.1 us (21%)
  local copies, waits for them, and re-layouts  79.9 us (20%)
  between operations  13.8 us (3%)
  other arithmetic  5.25 us (1%)
    all_to_all x1, blocking collectives, summed_on_arrival(): lax.all_to_all(pieces, axis, split_axis=0, concat_axis=0, tiled=True)  84.1 us
    all_gather x1, waiting for transfers between devices, in_one_piece(): whole, at, outs = (lax.all_gather(both, axis, axis=dim, tiled=True), 0, [])  62.5 us
    all_gather x1, waiting for transfers between devices, turned_gather(): whole, at, outs = (lax.all_gather(both, axis, axis=0, tiled=True), 0, [])  55.4 us
    dynamic_slice x64, local copies, waits for them, and re-layouts, columns(): lax.dynamic_slice_in_dim(source, column, pair_width, 1)  34.3 us
    dot_general x8, matrix products, head_pair(): jnp.einsum('qhd,khd->hqk', grads_out, values_pair, preferred_element_type...  26.8 us
    dot_general x8, matrix products, head_pair(): jnp.einsum('hqk,qhd->khd', probs_b, grads_out, preferred_element_type=jnp...  24.7 us
    dot_general x8, matrix products, head_pair(): jnp.einsum('qhd,khd->hqk', queries, keys_pair, preferred_element_type=jnp...  21.7 us
    dot_general x3, matrix products, project(): lax.dot_general(upper, weights, contract, preferred_element_type=jnp.floa...  11.4 us
  transfers between devices with their start and end apart: 3, of which 2 were waited for; matrix products, arithmetic and copies ran while one was open for 3% of the time, Pallas kernels for 0%

commit v1 on v0

--- a/solution.py
+++ b/solution.py
@@ -9,7 +9,13 @@
 def turned_gather(arrays, axis, dims):
     turned = [jnp.moveaxis(a, dim, 0) for a, dim in zip(arrays, dims)]
     both = jnp.concatenate([t.reshape(len(t), -1) for t in turned], axis=1)
-    whole, at, outs = (lax.all_gather(both, axis, axis=0, tiled=True), 0, [])
+    whole, at, outs = (
+        jnp.concatenate(
+            lax.all_to_all(jnp.stack([both] * lax.axis_size(axis)), axis, 0, 0), axis=0
+        ),
+        0,
+        [],
+    )
     for t, dim in zip(turned, dims):
         share = whole[:, at : at + t[0].size].reshape(-1, *t.shape[1:])
         outs.append(jnp.moveaxis(share, 0, dim))

time: 406 us -> 359 us (0.88)
  waiting for transfers between devices: 118 us -> 71.9 us
  blocking collectives: 84.1 us -> 69.8 us
  starting transfers between devices: 0.12 us -> 8.51 us
    all_to_all x0 -> x1, waiting for transfers between devices: none -> 71.9 us  [turned_gather(): lax.all_to_all(jnp.stack([both] * lax.axis_size(axis)), axis, 0, 0)]
    all_gather x1, waiting for transfers between devices: 62.5 us -> 0.01 us  [in_one_piece(): whole, at, outs = (lax.all_gather(both, axis, axis=dim, tiled=True), 0, [])]
    all_gather x1 -> x0, waiting for transfers between devices: 55.4 us -> none  [turned_gather(): whole, at, outs = (lax.all_gather(both, axis, axis=0, tiled=True), 0, [])]
    all_to_all x1, blocking collectives: 84.1 us -> 69.8 us  [summed_on_arrival(): lax.all_to_all(pieces, axis, split_axis=0, concat_axis=0, tiled=True)]
    all_to_all x0 -> x1, starting transfers between devices: none -> 8.44 us  [turned_gather(): lax.all_to_all(jnp.stack([both] * lax.axis_size(axis)), axis, 0, 0)]
  transfers between devices with their start and end apart: 3 -> 3, of which waited for: 2 -> 1; matrix products, arithmetic and copies ran while one was open for 3% -> 4% of each run, Pallas kernels for 0% -> 0%
where the time goes in v1:
time: 359 us; the launch traced here: 354 us
  matrix products  102 us (28%)
  local copies, waits for them, and re-layouts  80.6 us (22%)
  waiting for transfers between devices  71.9 us (20%)
  blocking collectives  69.8 us (19%)
  between operations  14.1 us (4%)
  starting transfers between devices  8.51 us (2%)
  other arithmetic  5.4 us (2%)
    all_to_all x1, waiting for transfers between devices, turned_gather(): lax.all_to_all(jnp.stack([both] * lax.axis_size(axis)), axis, 0, 0)  71.9 us
    all_to_all x1, blocking collectives, summed_on_arrival(): lax.all_to_all(pieces, axis, split_axis=0, concat_axis=0, tiled=True)  69.8 us
    dynamic_slice x64, local copies, waits for them, and re-layouts, columns(): lax.dynamic_slice_in_dim(source, column, pair_width, 1)  34.3 us
    dot_general x8, matrix products, head_pair(): jnp.einsum('qhd,khd->hqk', grads_out, values_pair, preferred_element_type...  26.8 us
    dot_general x8, matrix products, head_pair(): jnp.einsum('hqk,qhd->khd', probs_b, grads_out, preferred_element_type=jnp...  24.7 us
    dot_general x8, matrix products, head_pair(): jnp.einsum('qhd,khd->hqk', queries, keys_pair, preferred_element_type=jnp...  21.7 us
    dot_general x3, matrix products, project(): lax.dot_general(upper, weights, contract, preferred_element_type=jnp.floa...  11.4 us
    while x32, local copies, waits for them, and re-layouts  10.5 us
  transfers between devices with their start and end apart: 3, of which 1 were waited for; matrix products, arithmetic and copies ran while one was open for 4% of the time, Pallas kernels for 0%

profile of v1, /device:TPU:1, one launch (start us, length us, event | category | flops | bytes accessed | tf_op | source)
XLA Modules:
  0.0 353.8 jit_solution(9259513250507385075)
XLA Ops:
  13.2 8.4 %all-to-all-start = ((bf16[16,32,2080]{2,1,0:T(8,128)(2,1)}), bf16[16,32,2080]{2,1,0:T(8,128)(2,1)}, u32[]{:S(2)}, u32[]{:S(2)}) async-start(bf16[16,32,2080]{2,1,0:T(8,128)(2,1)} %stack.2), calls=%async_computation | async-start | bytes 4456448 | tf_op jit(solution)/shard_map/all_to_all | solution.py:14
  21.7 71.9 %all-to-all-done = bf16[16,32,2080]{2,1,0:T(8,128)(2,1)} async-done(((bf16[16,32,2080]{2,1,0:T(8,128)(2,1)}), bf16[16,32,2080]{2,1,0:T(8,128)(2,1)}, u32[]{:S(2)}, u32[]{:S(2)}) %all-to-all-start) | async-done | bytes 2129952 | tf_op jit(solution)/shard_map/all_to_all | solution.py:14
  94.8 3.1 fusion.20
  97.9 4.6 %fusion.19 = (bf16[1024,1024]{1,0:T(8,128)(2,1)}, bf16[1024,1024]{1,0:T(8,128)(2,1)}) fusion(bf16[1024,2048]{1,0:T(8,128)(2,1)} %all-gather.2.cloned.1.call-done), kind=kLoop, calls=%fused_computation.39 | loop fusion | bytes 8388608 | tf_op jit(solution)/shard_map/slice | solution.py:30
  109.0 145.0 %while.17 = (s32[]{:T(128)}, f32[512,1024]{1,0:T(8,128)}, f32[1024,1024]{0,1:T(8,128)}, f32[1024,1024]{0,1:T(8,128)}, bf16[1024,1024]{1,0:T(8,128)(2,1)}, /*inde...) while((s32[]{:T(128)}, f32[512,1024]{1,0:T(8,128)}, ...), condition=%wide.region_1.0_spmd, body=%wide.region_0.0_spmd.sunk | while | flops 679675904 | bytes 44589392 | solution.py:128
  111.2 2.7 fusion.61
  116.2 3.4 multiply_convert_fusion.2
  122.5 3.1 fusion.64
  129.3 2.7 fusion.61
  134.3 3.4 multiply_convert_fusion.2
  140.6 3.1 fusion.64
  147.4 2.7 fusion.61
  152.4 3.4 multiply_convert_fusion.2
  158.7 3.1 fusion.64
  170.5 3.4 multiply_convert_fusion.2
  176.8 3.1 fusion.64
  183.7 2.7 fusion.61
  188.6 3.4 multiply_convert_fusion.2
  195.0 3.1 fusion.64
  201.8 2.7 fusion.61
  206.7 3.4 multiply_convert_fusion.2
  213.1 3.1 fusion.64
  219.9 2.7 fusion.61
  224.9 3.4 multiply_convert_fusion.2
  231.2 3.1 fusion.64
  238.0 2.7 fusion.61
  243.0 3.4 multiply_convert_fusion.2
  249.3 3.1 fusion.64
  254.0 4.7 %fusion.14 = f32[1024,1024]{1,0:T(8,128)S(1)} fusion(bf16[1024,1024]{1,0:T(8,128)(2,1)S(1)} %copy-done, f32[1024,1024]{0,1:T(8,128)} %get-tuple-element.174), kind=kOutput, calls=%fused_computation.30 | convolution fusion | flops 2148532224 | bytes 10485760 | tf_op jit(solution)/shard_map/dot_general | solution.py:50
  264.0 4.4 %add_add_fusion = f32[1024,1024]{1,0:T(8,128)} fusion(f32[1024,1024]{1,0:T(8,128)S(1)} %fusion.9, f32[1024,1024]{1,0:T(8,128)S(1)} %fusion.14, f32[1024,1024]{1,0:T(8,128)S(1)} %fusion.8, bf16[1024,1024]{1,0:T(8,128)(2,1)S(1)} %copy-done.5, f32[1024,1024]{0,1:T(8,128)S(1)} %copy-done.3), kind=kOutput, calls=%fused_computation.20 | convolution fusion | flops 2151677952 | bytes 23068672 | tf_op jit(solution)/shard_map/dot_general | solution.py:50
  268.4 69.8 %all_to_all.10 = f32[16,32,1024]{2,1,0:T(8,128)} all-to-all(f32[16,32,1024]{2,1,0:T(8,128)} %bitcast.78), channel_id=1, replica_groups=mesh['pb'=16,'ka'=16] {'ka'}, dimensions={0} | all-to-all | bytes 4194304 | tf_op jit(solution)/shard_map/all_to_all | solution.py:42
  342.3 3.0 fusion.10
  (183 shorter events, 98.3 us)
Async XLA Ops:
  7.2 246.8 %copy-start = (bf16[1024,1024]{1,0:T(8,128)(2,1)S(1)}, bf16[1024,1024]{1,0:T(8,128)(2,1)}, u32[]{:S(2)}) copy-start(bf16[1024,1024]{1,0:T(8,128)(2,1)} %param.18) | copy-start | bytes 6291460
  7.2 90.7 %all-gather.2.cloned.1.call-start = ((), (), s32[]{:S(2)}) async-start(), calls=%async_computation.3 | async-start | bytes 4456448 | tf_op jit(solution)/shard_map/all_gather | solution.py:28
  13.2 80.4 %all-to-all-start = ((bf16[16,32,2080]{2,1,0:T(8,128)(2,1)}), bf16[16,32,2080]{2,1,0:T(8,128)(2,1)}, u32[]{:S(2)}, u32[]{:S(2)}) async-start(bf16[16,32,2080]{2,1,0:T(8,128)(2,1)} %stack.2), calls=%async_computation | async-start | bytes 4456448 | tf_op jit(solution)/shard_map/all_to_all | solution.py:14
  21.6 323.7 %reduce-scatter.2.cloned.1.call-start = ((), (), s32[]{:S(2)}) async-start(), calls=%async_computation.4 | async-start | bytes 4456448 | tf_op jit(solution)/shard_map/reduce_scatter | solution.py:131
  119.5 1.3 copy-start.1
  121.7 3.9 %copy-start.2 = (bf16[2,512,1024]{2,1,0:T(8,128)(2,1)S(1)}, bf16[2,512,1024]{2,1,0:T(8,128)(2,1)}, u32[]{:S(2)}) copy-start(bf16[2,512,1024]{2,1,0:T(8,128)(2,1)} %copy-done.1) | copy-start | bytes 6291460 | tf_op jit(solution)/shard_map/while
  137.6 1.3 copy-start.1
  139.8 3.9 %copy-start.2 = (bf16[2,512,1024]{2,1,0:T(8,128)(2,1)S(1)}, bf16[2,512,1024]{2,1,0:T(8,128)(2,1)}, u32[]{:S(2)}) copy-start(bf16[2,512,1024]{2,1,0:T(8,128)(2,1)} %copy-done.1) | copy-start | bytes 6291460 | tf_op jit(solution)/shard_map/while
  155.7 1.3 copy-start.1
  157.9 3.9 %copy-start.2 = (bf16[2,512,1024]{2,1,0:T(8,128)(2,1)S(1)}, bf16[2,512,1024]{2,1,0:T(8,128)(2,1)}, u32[]{:S(2)}) copy-start(bf16[2,512,1024]{2,1,0:T(8,128)(2,1)} %copy-done.1) | copy-start | bytes 6291460 | tf_op jit(solution)/shard_map/while
  173.9 1.3 copy-start.1
  176.1 3.9 %copy-start.2 = (bf16[2,512,1024]{2,1,0:T(8,128)(2,1)S(1)}, bf16[2,512,1024]{2,1,0:T(8,128)(2,1)}, u32[]{:S(2)}) copy-start(bf16[2,512,1024]{2,1,0:T(8,128)(2,1)} %copy-done.1) | copy-start | bytes 6291460 | tf_op jit(solution)/shard_map/while
  192.0 1.3 copy-start.1
  194.2 3.9 %copy-start.2 = (bf16[2,512,1024]{2,1,0:T(8,128)(2,1)S(1)}, bf16[2,512,1024]{2,1,0:T(8,128)(2,1)}, u32[]{:S(2)}) copy-start(bf16[2,512,1024]{2,1,0:T(8,128)(2,1)} %copy-done.1) | copy-start | bytes 6291460 | tf_op jit(solution)/shard_map/while
  210.1 1.3 copy-start.1
  212.3 3.9 %copy-start.2 = (bf16[2,512,1024]{2,1,0:T(8,128)(2,1)S(1)}, bf16[2,512,1024]{2,1,0:T(8,128)(2,1)}, u32[]{:S(2)}) copy-start(bf16[2,512,1024]{2,1,0:T(8,128)(2,1)} %copy-done.1) | copy-start | bytes 6291460 | tf_op jit(solution)/shard_map/while
  228.2 1.3 copy-start.1
  230.4 3.8 %copy-start.2 = (bf16[2,512,1024]{2,1,0:T(8,128)(2,1)S(1)}, bf16[2,512,1024]{2,1,0:T(8,128)(2,1)}, u32[]{:S(2)}) copy-start(bf16[2,512,1024]{2,1,0:T(8,128)(2,1)} %copy-done.1) | copy-start | bytes 6291460 | tf_op jit(solution)/shard_map/while
  246.3 1.3 copy-start.1
  248.5 3.9 %copy-start.2 = (bf16[2,512,1024]{2,1,0:T(8,128)(2,1)S(1)}, bf16[2,512,1024]{2,1,0:T(8,128)(2,1)}, u32[]{:S(2)}) copy-start(bf16[2,512,1024]{2,1,0:T(8,128)(2,1)} %copy-done.1) | copy-start | bytes 6291460 | tf_op jit(solution)/shard_map/while
  254.0 4.7 %copy-start.4 = (f32[1024,1024]{0,1:T(8,128)S(1)}, f32[1024,1024]{0,1:T(8,128)}, u32[]{:S(2)}) copy-start(f32[1024,1024]{0,1:T(8,128)} %get-tuple-element.174) | copy-start | bytes 12582916
  258.7 2.4 copy-start.3
  258.8 2.9 copy-start.5
Sparse Core Ops, SparseCore 0:
  9.8 71.3 all-gather.1
  268.6 70.8 reduce-scatter.1
